TPU v7x, 128 devices: a whole 4x4x4 slice. The times are simulated.
128 devices in a mesh: rep: 16 (over y_lo, z, core), shard: 8 (over x, y_hi).
Axes of the slice: x: 4, y: 4 (y_hi: 2, y_lo: 2; y = y_hi * 2 + y_lo), z: 4, core: 2. Of those that a mesh axis runs over, the one named last changes fastest.
Arguments:
- hidden_in: float32 [16384, 1024], P(('rep', 'shard')), may hold values from -6 to 6
- doc_start: int32 [16384], P(('rep', 'shard')), may hold values from 0 to 127, as said below
- grad_out: float32 [16384, 1024], P(('rep', 'shard')), may hold values from -6 to 6
- w_qkv: bfloat16 [2, 1024, 3072], P(None, 'shard'), may hold values from -0.1875 to 0.1875
- w_proj: bfloat16 [2, 1024, 1024], P(None, 'shard'), may hold values from -0.375 to 0.375
- w_up: bfloat16 [2, 1024, 4096], P(None, 'shard'), may hold values from -0.1875 to 0.1875
- w_down: bfloat16 [2, 4096, 1024], P(None, 'shard'), may hold values from -0.09375 to 0.09375
- norm_gain: bfloat16 [2, 1024, 2], P(None, 'shard'), may hold values from 0.5 to 1.5
- d_bias: bfloat16 [2, 1024, 6], P(None, 'shard'), may hold values from -3 to 3
- up_bias: bfloat16 [2, 4096], P(None, 'shard'), may hold values from -3 to 3
Outputs:
- hidden_out: float32 [16384, 1024], P(('rep', 'shard'))
- grad_in: float32 [16384, 1024], P(('rep', 'shard'))
- grad_qkv: float32 [2, 1024, 3072], P(None, 'shard')
- grad_proj: float32 [2, 1024, 1024], P(None, 'shard')
- grad_up: float32 [2, 1024, 4096], P(None, 'shard')
- grad_down: float32 [2, 4096, 1024], P(None, 'shard')
- grad_gain: float32 [2, 1024, 2], P(None, 'shard')
- grad_dbias: float32 [2, 1024, 6], P(None, 'shard')
- grad_upbias: float32 [2, 4096], P(None, 'shard')
Inputs may be any that keep to these rules, and one draw needn't show every extreme that they name: `doc_start`: each aligned run of 128 slots holds whole documents in order: the value does not fall along a run, is 0 at the run's first slot, and equals the slot's own offset at a document's first token.
All inputs are finite; a program needn't handle non-finite values.
Results may differ from a plain program's by a relative error of at most 0.025.
Values may be sent and summed in bfloat16 or wider, within the bound.
No kernel may reach another device: no remote copies, remote signals or barrier semaphores. Data moves between devices by JAX's collectives and lax.ppermute only.
A program may use at most 256 MiB of HBM per device.

v0:
```python
import jax
import jax.numpy as jnp
from jax import lax
from jax.sharding import PartitionSpec as P

HEADS = 16
HEAD_DIM = 64
LAYERS = 2
epsilon = 1e-05
gelu_coef = 0.7978845608


def in_one_piece(arrays, axis, dim, along):
    both = jnp.concatenate(arrays, axis=along)
    result, at, done = (lax.all_gather(both, axis, axis=dim, tiled=True), 0, [])
    for a in arrays:
        done.append(lax.slice_in_dim(result, at, at + a.shape[along], axis=along))
        at += a.shape[along]
    return tuple(done)


def split_up(shard, dim, length):
    shape = shard.shape
    tiles = shard.reshape(*shape[:dim], length, shape[dim] // length, *shape[dim + 1 :])
    return jnp.moveaxis(tiles, dim, 0)


def sent_and_summed(shard, axis, dim):
    length = lax.axis_size(axis)
    tiles = lax.all_to_all(split_up(shard, dim, length), axis, 0, 0, tiled=True)
    return jnp.sum(tiles.astype(jnp.float32), axis=0)


def sent_together(arrays, axis, dim, along):
    both = jnp.concatenate(arrays, axis=along)
    result, at, done = (sent_and_summed(both, axis, dim), 0, [])
    for a in arrays:
        done.append(lax.slice_in_dim(result, at, at + a.shape[along], axis=along))
        at += a.shape[along]
    return tuple(done)


def batch_prod(form, left, right):
    return jnp.einsum(form, left, right, preferred_element_type=jnp.float32)


def layer_norm(stream, gains, shifts):
    average = jnp.mean(stream, axis=-1, keepdims=True)
    centered = stream - average
    variance = jnp.mean(centered * centered, axis=-1, keepdims=True)
    inv_std = lax.rsqrt(variance + epsilon)
    normed = centered * inv_std
    return (normed * gains + shifts, normed, inv_std)


def norm_back(grad_norm, normed, inv_std, gains):
    scaled = grad_norm * gains
    inner = (
        scaled
        - jnp.mean(scaled, axis=-1, keepdims=True)
        - normed * jnp.mean(scaled * normed, axis=-1, keepdims=True)
    )
    return (inv_std * inner, jnp.sum(grad_norm * normed, axis=0), jnp.sum(grad_norm, axis=0))


def gelu_tanh(values):
    inner = jnp.tanh(gelu_coef * (values + 0.044715 * values * values * values))
    return 0.5 * values * (1.0 + inner)


def gelu_slope(values):
    inner = jnp.tanh(gelu_coef * (values + 0.044715 * values * values * values))
    return 0.5 * (1.0 + inner) + 0.5 * values * (1.0 - inner * inner) * gelu_coef * (
        1.0 + 3.0 * 0.044715 * values * values
    )


def scores_of(query, keys_bf, starts):
    count = query.shape[0]
    query_heads = query.reshape(count, HEADS, HEAD_DIM)
    key_heads = keys_bf.reshape(count, HEADS, HEAD_DIM)
    scores = batch_prod("qhd,khd->hqk", query_heads, key_heads) * HEAD_DIM ** (-0.5)
    offsets = jnp.arange(count, dtype=jnp.int32)
    distance = (offsets[:, None] - offsets[None, :]).astype(jnp.float32)
    head_ids = jnp.arange(HEADS, dtype=jnp.int32).astype(jnp.float32)
    slopes = 2.0 ** (-8.0 * (head_ids + 1.0) / HEADS)
    scores = scores - slopes[:, None, None] * distance[None, :, :]
    visible = (starts[:, None] == starts[None, :]) & (offsets[None, :] <= offsets[:, None])
    return jnp.where(visible[None, :, :], scores, jnp.float32(-1000000000.0))


def layer_forward(stream, starts, wqkv, wproj, wupper, wlower, gains, biases, ubias):
    count, width = stream.shape
    gains = gains.astype(jnp.float32)
    biases = biases.astype(jnp.float32)
    first_f, normed_one, inv_one = layer_norm(stream, gains[:, 0], biases[:, 0])
    first_in = first_f.astype(jnp.bfloat16)
    merged = jnp.dot(first_in, wqkv, preferred_element_type=jnp.float32)
    query = (merged[:, :width] + biases[:, 2]).astype(jnp.bfloat16)
    keys_bf = merged[:, width : 2 * width].astype(jnp.bfloat16)
    values_bf = (merged[:, 2 * width :] + biases[:, 3]).astype(jnp.bfloat16)
    scores = scores_of(query, keys_bf, starts)
    top_score = jnp.max(scores, axis=-1, keepdims=True)
    log_total = top_score + jnp.log(jnp.sum(jnp.exp(scores - top_score), axis=-1, keepdims=True))
    weights_bf = jnp.exp(scores - log_total).astype(jnp.bfloat16)
    context = batch_prod("hqk,khd->qhd", weights_bf, values_bf.reshape(count, HEADS, HEAD_DIM))
    context = context.reshape(count, width).astype(jnp.bfloat16)
    middle = stream + jnp.dot(context, wproj, preferred_element_type=jnp.float32) + biases[:, 4]
    second_f, normed_two, inv_two = layer_norm(middle, gains[:, 1], biases[:, 1])
    second_in = second_f.astype(jnp.bfloat16)
    upper = jnp.dot(second_in, wupper, preferred_element_type=jnp.float32) + ubias.astype(
        jnp.float32
    )
    activ = gelu_tanh(upper).astype(jnp.bfloat16)
    result = middle + jnp.dot(activ, wlower, preferred_element_type=jnp.float32) + biases[:, 5]
    kept = (
        first_in,
        normed_one,
        inv_one,
        query,
        keys_bf,
        values_bf,
        log_total,
        context,
        second_in,
        normed_two,
        inv_two,
        upper,
        activ,
    )
    return (result, kept)


def layer_backward(
    grad_y, starts, kept, wqkv, wproj, wupper, wlower, gains, biases, ubias, full_terms
):
    (
        first_in,
        normed_one,
        inv_one,
        query,
        keys_bf,
        values_bf,
        log_total,
        context,
        second_in,
        normed_two,
        inv_two,
        upper,
        activ,
    ) = kept
    count, width = grad_y.shape
    gains = gains.astype(jnp.float32)
    grad_yb = grad_y.astype(jnp.bfloat16)
    g_bdown = jnp.sum(grad_y, axis=0)
    grad_act = jnp.dot(grad_yb, wlower.T, preferred_element_type=jnp.float32)
    grad_upper = grad_act * gelu_slope(upper)
    g_ubias = jnp.sum(grad_upper, axis=0)
    grad_ub = grad_upper.astype(jnp.bfloat16)
    grad_two = jnp.dot(grad_ub, wupper.T, preferred_element_type=jnp.float32)
    back_two, g_gain_two, g_shift_two = norm_back(grad_two, normed_two, inv_two, gains[:, 1])
    grad_mid = grad_y + back_two
    grad_midb = grad_mid.astype(jnp.bfloat16)
    g_bproj = jnp.sum(grad_mid, axis=0)
    grad_ctx = jnp.dot(grad_midb, wproj.T, preferred_element_type=jnp.float32).astype(jnp.bfloat16)
    scores = scores_of(query, keys_bf, starts)
    probs = jnp.exp(scores - log_total)
    probs_bf = probs.astype(jnp.bfloat16)
    ctx_heads = grad_ctx.reshape(count, HEADS, HEAD_DIM)
    grad_val = batch_prod("hqk,qhd->khd", probs_bf, ctx_heads)
    grad_prob = batch_prod("qhd,khd->hqk", ctx_heads, values_bf.reshape(count, HEADS, HEAD_DIM))
    delta = jnp.sum(
        ctx_heads.astype(jnp.float32) * context.reshape(count, HEADS, HEAD_DIM).astype(jnp.float32),
        axis=-1,
    )
    grad_score = (probs * (grad_prob - jnp.transpose(delta)[:, :, None])).astype(jnp.bfloat16)
    grad_query = batch_prod(
        "hqk,khd->qhd", grad_score, keys_bf.reshape(count, HEADS, HEAD_DIM)
    ) * HEAD_DIM ** (-0.5)
    grad_key = batch_prod(
        "hqk,qhd->khd", grad_score, query.reshape(count, HEADS, HEAD_DIM)
    ) * HEAD_DIM ** (-0.5)
    grad_query = grad_query.reshape(count, width)
    grad_key = grad_key.reshape(count, width)
    grad_val = grad_val.reshape(count, width)
    g_bquery = jnp.sum(grad_query, axis=0)
    g_bvalue = jnp.sum(grad_val, axis=0)
    grad_merged = jnp.concatenate([grad_query, grad_key, grad_val], axis=1).astype(jnp.bfloat16)
    grad_one = jnp.dot(grad_merged, wqkv.T, preferred_element_type=jnp.float32)
    back_one, g_gain_one, g_shift_one = norm_back(grad_one, normed_one, inv_one, gains[:, 0])
    grad_x = grad_mid + back_one
    g_gain = jnp.stack([g_gain_one, g_gain_two], axis=1)
    g_bias = jnp.stack([g_shift_one, g_shift_two, g_bquery, g_bvalue, g_bproj, g_bdown], axis=1)
    g_down, g_up, g_proj, g_qkv = (None, None, None, None)
    operands = (grad_yb, grad_ub, grad_midb, grad_merged)
    return (grad_x, (g_qkv, g_proj, g_up, g_down, g_gain, g_bias, g_ubias), operands)


def local(hidden_in, doc_start, grad_out, w_qkv, w_proj, w_up, w_down, norm_gain, d_bias, up_bias):
    saved = []
    current = hidden_in
    for layer_no in range(LAYERS):
        whole = (
            *in_one_piece((w_qkv[layer_no], w_proj[layer_no], w_up[layer_no]), "shard", 0, 1),
            lax.all_gather(w_down[layer_no], "shard", axis=0, tiled=True),
            *in_one_piece((norm_gain[layer_no], d_bias[layer_no]), "shard", 0, 1),
            lax.all_gather(up_bias[layer_no], "shard", axis=0, tiled=True),
        )
        current, kept = layer_forward(current, doc_start, *whole)
        saved.append(kept)
    running = grad_out
    owned = [None] * LAYERS
    for layer_no in reversed(range(LAYERS)):
        whole = (
            *in_one_piece((w_qkv[layer_no], w_proj[layer_no], w_up[layer_no]), "shard", 0, 1),
            lax.all_gather(w_down[layer_no], "shard", axis=0, tiled=True),
            *in_one_piece((norm_gain[layer_no], d_bias[layer_no]), "shard", 0, 1),
            lax.all_gather(up_bias[layer_no], "shard", axis=0, tiled=True),
        )
        kept = saved[layer_no]
        running, terms, operands = layer_backward(running, doc_start, kept, *whole, False)
        joined = in_one_piece((operands[0], operands[1], operands[2], operands[3]), "shard", 0, 1)
        pieces = (
            lax.all_to_all(kept[0], "shard", split_axis=1, concat_axis=0, tiled=True),
            lax.all_to_all(kept[7], "shard", split_axis=1, concat_axis=0, tiled=True),
            lax.all_to_all(kept[8], "shard", split_axis=1, concat_axis=0, tiled=True),
            lax.all_to_all(kept[12], "shard", split_axis=1, concat_axis=0, tiled=True),
        )
        own_qkv = jnp.dot(pieces[0].T, joined[3], preferred_element_type=jnp.float32)
        own_proj = jnp.dot(pieces[1].T, joined[2], preferred_element_type=jnp.float32)
        own_up = jnp.dot(pieces[2].T, joined[1], preferred_element_type=jnp.float32)
        own_down = jnp.dot(pieces[3].T, joined[0], preferred_element_type=jnp.float32)
        small = (
            *sent_together(
                (terms[4].astype(jnp.bfloat16), terms[5].astype(jnp.bfloat16)), "shard", 0, 1
            ),
            sent_and_summed(terms[6].astype(jnp.bfloat16), "shard", 0),
        )
        shares = (own_qkv, own_proj, own_up, own_down, small[0], small[1], small[2])
        shares = (
            lax.psum(shares[0].astype(jnp.bfloat16), "rep").astype(jnp.float32),
            lax.psum(shares[1].astype(jnp.bfloat16), "rep").astype(jnp.float32),
            lax.psum(shares[2].astype(jnp.bfloat16), "rep").astype(jnp.float32),
            lax.psum(shares[3].astype(jnp.bfloat16), "rep").astype(jnp.float32),
            lax.psum(shares[4].astype(jnp.bfloat16), "rep").astype(jnp.float32),
            lax.psum(shares[5].astype(jnp.bfloat16), "rep").astype(jnp.float32),
            lax.psum(shares[6].astype(jnp.bfloat16), "rep").astype(jnp.float32),
        )
        owned[layer_no] = shares
    stacked = [
        jnp.stack([owned[layer_no][slot] for layer_no in range(LAYERS)]) for slot in range(7)
    ]
    return (
        current,
        running,
        stacked[0],
        stacked[1],
        stacked[2],
        stacked[3],
        stacked[4],
        stacked[5],
        stacked[6],
    )


def solution(mesh):
    placed = (
        P(("rep", "shard"), None),
        P(("rep", "shard")),
        P(("rep", "shard"), None),
        P(None, "shard", None),
        P(None, "shard", None),
        P(None, "shard", None),
        P(None, "shard", None),
        P(None, "shard", None),
        P(None, "shard", None),
        P(None, "shard"),
    )
    return jax.shard_map(
        local,
        mesh=mesh,
        in_specs=placed,
        out_specs=(
            P(("rep", "shard"), None),
            P(("rep", "shard"), None),
            P(None, "shard", None),
            P(None, "shard", None),
            P(None, "shard", None),
            P(None, "shard", None),
            P(None, "shard", None),
            P(None, "shard", None),
            P(None, "shard"),
        ),
        check_vma=False,
    )
```

profile of v0, /device:TPU:0, one launch (start us, length us, event | category | flops | bytes accessed | tf_op | source)
XLA Modules:
  0.0 1301.5 jit_solution(16757099356191935756)
XLA Ops:
  17.2 30.1 %all-gather = bf16[1,4096]{1,0:T(2,128)(2,1)S(1)} all-gather(bf16[1,512]{1,0:T(2,128)(2,1)S(1)} %get-tuple-element.107), channel_id=2, replica_groups=mesh['rep'=16,'shard'=8] {'shard'}, dimensions={1}, use_global_device_ids=true | all-gather | bytes 9216 | tf_op jit(solution)/shard_map/all_gather | solution.py:207
  47.4 29.7 %all-gather.2 = bf16[1,4096]{1,0:T(2,128)(2,1)S(1)} all-gather(bf16[1,512]{1,0:T(2,128)(2,1)S(1)} %get-tuple-element.106), channel_id=4, replica_groups=mesh['rep'=16,'shard'=8] {'shard'}, dimensions={1}, use_global_device_ids=true | all-gather | bytes 9216 | tf_op jit(solution)/shard_map/all_gather | solution.py:207
  77.2 29.7 %all_gather.36 = bf16[1024,8]{0,1:T(8,128)(2,1)S(1)} all-gather(bf16[128,8]{0,1:T(8,128)(2,1)S(1)} %pad_maximum_fusion.2), channel_id=1, replica_groups=mesh['rep'=16,'shard'=8] {'shard'}, dimensions={0}, use_global_device_ids=true | all-gather | bytes 18432 | tf_op jit(solution)/shard_map/all_gather | solution.py:15
  107.0 29.8 %all_gather.40 = bf16[1024,8]{0,1:T(8,128)(2,1)S(1)} all-gather(bf16[128,8]{0,1:T(8,128)(2,1)S(1)} %pad_maximum_fusion.3), channel_id=1, replica_groups=mesh['rep'=16,'shard'=8] {'shard'}, dimensions={0}, use_global_device_ids=true | all-gather | bytes 18432 | tf_op jit(solution)/shard_map/all_gather | solution.py:15
  138.0 63.1 %all-gather.11.cloned.1.call-done = bf16[1024,8192]{1,0:T(8,128)(2,1)} async-done(((bf16[128,8192]{1,0:T(8,128)(2,1)}), bf16[1024,8192]{1,0:T(8,128)(2,1)}) %all-gather.11.cloned.1.call-update) | async-done | bytes 16777232 | tf_op jit(solution)/shard_map/all_gather | solution.py:15
  209.0 7.7 multiply_convert_fusion.1
  216.7 93.6 %all-gather.19.cloned.1.call-done = bf16[1,4096,1024]{2,1,0:T(8,128)(2,1)} async-done(((bf16[1,512,1024]{2,1,0:T(8,128)(2,1)}), bf16[1,4096,1024]{2,1,0:T(8,128)(2,1)}) %all-gather.19.cloned.1.call-update) | async-done | bytes 8388624 | tf_op jit(solution)/shard_map/all_gather | solution.py:205
  315.6 181.5 %all-gather.13.cloned.1.call-done = bf16[1024,8192]{1,0:T(8,128)(2,1)} async-done(((bf16[128,8192]{1,0:T(8,128)(2,1)}), bf16[1024,8192]{1,0:T(8,128)(2,1)}) %all-gather.13.cloned.1.call-update) | async-done | bytes 16777232 | tf_op jit(solution)/shard_map/all_gather | solution.py:15
  506.8 7.7 multiply_convert_fusion
  514.4 91.6 %all-gather.21.cloned.1.call-done = bf16[1,4096,1024]{2,1,0:T(8,128)(2,1)} async-done(((bf16[1,512,1024]{2,1,0:T(8,128)(2,1)}), bf16[1,4096,1024]{2,1,0:T(8,128)(2,1)}) %all-gather.21.cloned.1.call-update) | async-done | bytes 8388624 | tf_op jit(solution)/shard_map/all_gather | solution.py:205
  606.1 8.7 convert_dynamic-update-slice_fusion.1
  614.8 7.0 fusion.12
  643.5 8.1 fusion.16
  674.5 8.5 all-to-all-done.4
  716.0 168.9 %all-gather.15.cloned.1.call-done = bf16[1024,9216]{1,0:T(8,128)(2,1)} async-done(((bf16[128,9216]{1,0:T(8,128)(2,1)}), bf16[1024,9216]{1,0:T(8,128)(2,1)}) %all-gather.15.cloned.1.call-update) | async-done | bytes 18874384 | tf_op jit(solution)/shard_map/all_gather | solution.py:15
  889.7 5.6 fusion.53
  903.9 198.0 %all-gather.17.cloned.1.call-done = bf16[1024,9216]{1,0:T(8,128)(2,1)} async-done(((bf16[128,9216]{1,0:T(8,128)(2,1)}), bf16[1024,9216]{1,0:T(8,128)(2,1)}) %all-gather.17.cloned.1.call-update) | async-done | bytes 18874384 | tf_op jit(solution)/shard_map/all_gather | solution.py:15
  1101.9 5.7 fusion.50
  1164.8 7.1 all-to-all-start.11
  1172.5 7.1 all-to-all-done.11
  1183.6 7.0 all-to-all-done.8
  1195.1 6.4 all-to-all-done.9
  1201.6 28.4 %all-reduce = (bf16[1,128,2]{1,2,0:T(2,128)(2,1)S(1)}, bf16[1,128,2]{1,2,0:T(2,128)(2,1)S(1)}, bf16[1,128,6]{1,2,0:T(8,128)(2,1)S(1)}, bf16[1,128,6]{1,2,0:T(8,1...) all-reduce(bf16[1,128,2]{1,2,0:T(2,128)(2,1)S(1)} %slice_bitcast_fu, ...), channel_id=1, replica_groups=mesh['rep'=16,'shard'=8] {'rep'}, use_global_device_ids=true, to_apply=%region_49.50 | all-reduce | flops 3072 | bytes 12288 | tf_op jit(solution)/shard_map/psum | solution.py:245
  1231.8 52.5 %all-reduce.4.cloned.1.call-done = (bf16[1,128,3072]{2,1,0:T(8,128)(2,1)}, bf16[1,128,3072]{2,1,0:T(8,128)(2,1)}, bf16[1,128,1024]{2,1,0:T(8,128)(2,1)}, bf16[1,...) async-done(((bf16[1,128,3072]{2,1,0:T(8,128)(2,1)}, ...) | async-done | bytes 6291472 | tf_op jit(solution)/shard_map/psum | solution.py:241
  (368 shorter events, 201.9 us)
Async XLA Ops:
  7.2 194.0 %all-gather.11.cloned.1.call-start = ((), (), s32[]{:S(2)}) async-start(), calls=%async_computation.12 | async-start | bytes 18874368 | tf_op jit(solution)/shard_map/all_gather | solution.py:15
  11.8 298.5 %all-gather.19.cloned.1.call-start = ((), (), s32[]{:S(2)}) async-start(), calls=%async_computation.16 | async-start | bytes 9437184 | tf_op jit(solution)/shard_map/all_gather | solution.py:205
  15.0 482.1 %all-gather.13.cloned.1.call-start = ((), (), s32[]{:S(2)}) async-start(), calls=%async_computation.13 | async-start | bytes 18874368 | tf_op jit(solution)/shard_map/all_gather | solution.py:15
  16.5 120.6 %copy-start.69 = (s32[128]{0:T(128)S(1)}, s32[128]{0:T(128)}, u32[]{:S(2)}) copy-start(s32[128]{0:T(128)} %param.11) | copy-start | bytes 1540
  16.5 120.8 %copy-start.21 = (f32[128,1024]{1,0:T(8,128)S(1)}, f32[128,1024]{1,0:T(8,128)}, u32[]{:S(2)}) copy-start(f32[128,1024]{1,0:T(8,128)} %param.12) | copy-start | bytes 1572868
  16.5 589.5 %all-gather.21.cloned.1.call-start = ((), (), s32[]{:S(2)}) async-start(), calls=%async_computation.17 | async-start | bytes 9437184 | tf_op jit(solution)/shard_map/all_gather | solution.py:205
  17.1 867.7 %all-gather.15.cloned.1.call-start = ((), (), s32[]{:S(2)}) async-start(), calls=%async_computation.14 | async-start | bytes 21233664 | tf_op jit(solution)/shard_map/all_gather | solution.py:15
  315.3 185.6 %copy-start.3 = (f32[128,1024]{1,0:T(8,128)}, f32[128,1024]{1,0:T(8,128)S(1)}, u32[]{:S(2)}) copy-start(f32[128,1024]{1,0:T(8,128)S(1)} %get-tuple-element.117) | copy-start | bytes 1572868
  315.4 185.6 %copy-start.65 = (f32[128]{0:T(128)}, f32[128]{0:T(128)S(1)}, u32[]{:S(2)}) copy-start(f32[128]{0:T(128)S(1)} %broadcast_multiply_fusion.9) | copy-start | bytes 1540
  315.6 185.3 %copy-start.72 = (f32[128]{0:T(128)}, f32[128]{0:T(128)S(1)}, u32[]{:S(2)}) copy-start(f32[128]{0:T(128)S(1)} %add_rsqrt_fusion.1) | copy-start | bytes 1540
  665.6 436.3 %all-gather.17.cloned.1.call-start = ((), (), s32[]{:S(2)}) async-start(), calls=%async_computation.15 | async-start | bytes 21233664 | tf_op jit(solution)/shard_map/all_gather | solution.py:15
  670.3 12.7 all-to-all-start.4
  683.0 14.2 %all-to-all-start.5 = ((bf16[128,8,128]{2,0,1:T(8,128)(2,1)}), bf16[128,8,128]{2,0,1:T(8,128)(2,1)}, u32[]{:S(2)}, u32[]{:S(2)}) async-start(bf16[128,8,128]{2,0,1:T(8,128)(2,1)} %bitcast.236), calls=%async_computation.5 | async-start | bytes 524288 | tf_op jit(solution)/shard_map/all_to_all | solution.py:226
  697.2 14.3 %all-to-all-start = ((bf16[128,8,128]{2,0,1:T(8,128)(2,1)}), bf16[128,8,128]{2,0,1:T(8,128)(2,1)}, u32[]{:S(2)}, u32[]{:S(2)}) async-start(bf16[128,8,128]{2,0,1:T(8,128)(2,1)} %bitcast.263), calls=%async_computation | async-start | bytes 524288 | tf_op jit(solution)/shard_map/all_to_all | solution.py:224
  711.5 183.8 %all-to-all-start.6 = ((bf16[128,8,512]{2,0,1:T(8,128)(2,1)}), bf16[128,8,512]{2,0,1:T(8,128)(2,1)}, u32[]{:S(2)}, u32[]{:S(2)}) async-start(bf16[128,8,512]{2,0,1:T(8,128)(2,1)} %bitcast.235), calls=%async_computation.6 | async-start | bytes 2097152 | tf_op jit(solution)/shard_map/all_to_all | solution.py:227
  895.3 212.3 %all-to-all-start.7 = ((bf16[128,8,512]{2,0,1:T(8,128)(2,1)}), bf16[128,8,512]{2,0,1:T(8,128)(2,1)S(1)}, u32[]{:S(2)}, u32[]{:S(2)}) async-start(bf16[128,8,512]{2,0,1:T(8,128)(2,1)} %bitcast.234), calls=%async_computation.7 | async-start | bytes 2097152 | tf_op jit(solution)/shard_map/all_to_all | solution.py:227
  1108.6 11.9 all-to-all-start.2
  1120.5 11.8 all-to-all-start.3
  1132.3 11.8 all-to-all-start.1
  1135.7 148.5 %all-reduce.4.cloned.1.call-start = ((), (), s32[]{:S(2)}) async-start(), calls=%async_computation.18 | async-start | bytes 12582912 | tf_op jit(solution)/shard_map/psum | solution.py:241
  1152.7 12.1 all-to-all-start.10
  1164.8 14.8 %all-to-all-start.11 = ((bf16[8,2,256]{2,1,0:T(2,128)(2,1)}), bf16[8,2,256]{2,1,0:T(2,128)(2,1)S(1)}, u32[]{:S(2)}, u32[]{:S(2)}) async-start(bf16[8,2,256]{2,1,0:T(2,128)(2,1)} %reshape.400), calls=%async_computation.11 | async-start | bytes 16384 | tf_op jit(solution)/shard_map/all_to_all | solution.py:30
  1179.6 11.0 all-to-all-start.8
  1190.6 11.0 all-to-all-start.9
  (74 other events, 794.3 us)
Sparse Core Ops, SparseCore 0:
  11.9 189.1 all-gather.10
  203.5 106.7 all-gather.18
  313.2 183.8 all-gather.12
  499.2 106.7 all-gather.20
  665.7 219.1 all-gather.14
  887.6 214.2 all-gather.16
  1148.9 135.2 all-reduce.3
where the time goes:
time: 1310 us; the launch traced here: 1300 us
  waiting for transfers between devices  903 us (69%)
  blocking collectives  148 us (11%)
  matrix products  127 us (10%)
  starting transfers between devices  47.8 us (4%)
  local copies, waits for them, and re-layouts  32.1 us (2%)
  other arithmetic  28.6 us (2%)
  between operations  16 us (1%)
    all_gather x4, waiting for transfers between devices, in_one_piece(): result, at, done = (lax.all_gather(both, axis, axis=dim, tiled=True), 0, [])  611 us
    all_gather x2, waiting for transfers between devices, local(): lax.all_gather(w_down[layer_no], 'shard', axis=0, tiled=True)  185 us
    all_gather x2, blocking collectives, local(): lax.all_gather(up_bias[layer_no], 'shard', axis=0, tiled=True)  59.8 us
    all_gather x2, blocking collectives, in_one_piece(): result, at, done = (lax.all_gather(both, axis, axis=dim, tiled=True), 0, [])  59.5 us
    psum x1, waiting for transfers between devices, local(): lax.psum(shares[0].astype(jnp.bfloat16), 'rep').astype(jnp.float32)  52.5 us
    psum x1, blocking collectives, local(): lax.psum(shares[4].astype(jnp.bfloat16), 'rep').astype(jnp.float32)  28.4 us
  transfers between devices with their start and end apart: 19, of which 16 were waited for; matrix products, arithmetic and copies ran while one was open for 8% of the time, Pallas kernels for 0%

commit v1 on v0

--- a/solution.py
+++ b/solution.py
@@ -202,7 +202,12 @@
     for layer_no in range(LAYERS):
         whole = (
             *in_one_piece((w_qkv[layer_no], w_proj[layer_no], w_up[layer_no]), "shard", 0, 1),
-            lax.all_gather(w_down[layer_no], "shard", axis=0, tiled=True),
+            jnp.concatenate(
+                lax.all_to_all(
+                    jnp.stack([w_down[layer_no]] * lax.axis_size("shard")), "shard", 0, 0
+                ),
+                axis=0,
+            ),
             *in_one_piece((norm_gain[layer_no], d_bias[layer_no]), "shard", 0, 1),
             lax.all_gather(up_bias[layer_no], "shard", axis=0, tiled=True),
         )

time: 1310 us -> 1460 us (1.11)
  blocking collectives: 148 us -> 304 us
  waiting for transfers between devices: 903 us -> 876 us
    all_gather x2, blocking collectives: 59.8 us -> 197 us  [local(): lax.all_gather(up_bias[layer_no], 'shard', axis=0, tiled=True)]
    all_gather x4, waiting for transfers between devices: 611 us -> 568 us  [in_one_piece(): result, at, done = (lax.all_gather(both, axis, axis=dim, tiled=True), 0, [])]
    all_to_all x2 -> x1, waiting for transfers between devices: 0.01 us -> 23 us  [local(): lax.all_to_all(kept[12], 'shard', split_axis=1, concat_axis=0, tiled=True)]
    all_to_all x0 -> x1, blocking collectives: none -> 19.5 us  [local(): lax.all_to_all(kept[12], 'shard', split_axis=1, concat_axis=0, tiled=True)]
    all_gather x2, waiting for transfers between devices: 185 us -> 166 us  [local(): lax.all_gather(w_down[layer_no], 'shard', axis=0, tiled=True)]
  transfers between devices with their start and end apart: 19 -> 20, of which waited for: 16 -> 17; matrix products, arithmetic and copies ran while one was open for 8% -> 10% of each run, Pallas kernels for 0% -> 0%
where the time goes in v1:
time: 1460 us
  waiting for transfers between devices  876 us (60%)
  blocking collectives  304 us (21%)
  matrix products  128 us (9%)
  starting transfers between devices  58.5 us (4%)
  local copies, waits for them, and re-layouts  42.4 us (3%)
  other arithmetic  30.3 us (2%)
  between operations  15.7 us (1%)
    all_gather x4, waiting for transfers between devices, in_one_piece(): result, at, done = (lax.all_gather(both, axis, axis=dim, tiled=True), 0, [])  568 us
    all_gather x2, blocking collectives, local(): lax.all_gather(up_bias[layer_no], 'shard', axis=0, tiled=True)  197 us
    all_gather x2, waiting for transfers between devices, local(): lax.all_gather(w_down[layer_no], 'shard', axis=0, tiled=True)  166 us
    all_gather x2, blocking collectives, in_one_piece(): result, at, done = (lax.all_gather(both, axis, axis=dim, tiled=True), 0, [])  59.6 us
    psum x1, waiting for transfers between devices, local(): lax.psum(shares[0].astype(jnp.bfloat16), 'rep').astype(jnp.float32)  52.9 us
  transfers between devices with their start and end apart: 20, of which 17 were waited for; matrix products, arithmetic and copies ran while one was open for 10% of the time, Pallas kernels for 0%

profile of v1, /device:TPU:0, one launch (start us, length us, event | category | flops | bytes accessed | tf_op | source)
XLA Modules:
  0.0 1455.1 jit_solution(18174794522141802623)
XLA Ops:
  29.1 167.1 %all-gather = bf16[1,4096]{1,0:T(2,128)(2,1)S(1)} all-gather(bf16[1,512]{1,0:T(2,128)(2,1)S(1)} %get-tuple-element.109), channel_id=2, replica_groups=mesh['rep'=16,'shard'=8] {'shard'}, dimensions={1}, use_global_device_ids=true | all-gather | bytes 9216 | tf_op jit(solution)/shard_map/all_gather | solution.py:212
  196.2 29.8 %all-gather.1 = bf16[1,4096]{1,0:T(2,128)(2,1)S(1)} all-gather(bf16[1,512]{1,0:T(2,128)(2,1)S(1)} %get-tuple-element.108), channel_id=3, replica_groups=mesh['rep'=16,'shard'=8] {'shard'}, dimensions={1}, use_global_device_ids=true | all-gather | bytes 9216 | tf_op jit(solution)/shard_map/all_gather | solution.py:212
  226.1 29.7 %all_gather.34 = bf16[1024,8]{0,1:T(8,128)(2,1)S(1)} all-gather(bf16[128,8]{0,1:T(8,128)(2,1)S(1)} %pad_maximum_fusion.2), channel_id=1, replica_groups=mesh['rep'=16,'shard'=8] {'shard'}, dimensions={0}, use_global_device_ids=true | all-gather | bytes 18432 | tf_op jit(solution)/shard_map/all_gather | solution.py:15
  255.8 29.9 %all_gather.37 = bf16[1024,8]{0,1:T(8,128)(2,1)S(1)} all-gather(bf16[128,8]{0,1:T(8,128)(2,1)S(1)} %pad_maximum_fusion.3), channel_id=1, replica_groups=mesh['rep'=16,'shard'=8] {'shard'}, dimensions={0}, use_global_device_ids=true | all-gather | bytes 18432 | tf_op jit(solution)/shard_map/all_gather | solution.py:15
  287.0 16.7 %all-gather.11.cloned.1.call-done = bf16[1024,8192]{1,0:T(8,128)(2,1)} async-done(((bf16[128,8192]{1,0:T(8,128)(2,1)}), bf16[1024,8192]{1,0:T(8,128)(2,1)}) %all-gather.11.cloned.1.call-update) | async-done | bytes 16777232 | tf_op jit(solution)/shard_map/all_gather | solution.py:15
  311.6 8.0 multiply_convert_fusion.1
  324.9 165.0 %all-gather.13.cloned.1.call-done = bf16[1024,8192]{1,0:T(8,128)(2,1)} async-done(((bf16[128,8192]{1,0:T(8,128)(2,1)}), bf16[1024,8192]{1,0:T(8,128)(2,1)}) %all-gather.13.cloned.1.call-update) | async-done | bytes 16777232 | tf_op jit(solution)/shard_map/all_gather | solution.py:15
  499.6 7.8 multiply_convert_fusion
  507.4 91.7 %all-gather.19.cloned.1.call-done = bf16[1,4096,1024]{2,1,0:T(8,128)(2,1)} async-done(((bf16[1,512,1024]{2,1,0:T(8,128)(2,1)}), bf16[1,4096,1024]{2,1,0:T(8,128)(2,1)}) %all-gather.19.cloned.1.call-update) | async-done | bytes 8388624 | tf_op jit(solution)/shard_map/all_gather | solution.py:221
  599.1 8.7 convert_dynamic-update-slice_fusion.1
  607.9 7.8 fusion.8
  634.0 74.1 %all-gather.21.cloned.1.call-done = bf16[1,4096,1024]{2,1,0:T(8,128)(2,1)} async-done(((bf16[1,512,1024]{2,1,0:T(8,128)(2,1)}), bf16[1,4096,1024]{2,1,0:T(8,128)(2,1)}) %all-gather.21.cloned.1.call-update) | async-done | bytes 8388624 | tf_op jit(solution)/shard_map/all_gather | solution.py:221
  708.1 8.4 convert_dynamic-update-slice_fusion
  716.6 7.4 fusion.12
  751.0 7.8 all-to-all-done.6
  763.0 9.3 all-to-all-done.7
  777.7 9.1 all-to-all-done.4
  819.1 8.7 all-to-all-done.3
  833.3 23.0 %all-to-all-done.8 = bf16[128,8,512]{2,0,1:T(8,128)(2,1)} async-done(((bf16[128,8,512]{2,0,1:T(8,128)(2,1)}), bf16[128,8,512]{2,0,1:T(8,128)(2,1)}, u32[]{:S(2)}, u32[]{:S(2)}) %all-to-all-start.8) | async-done | bytes 1048608 | tf_op jit(solution)/shard_map/all_to_all | solution.py:232
  856.4 19.5 %all_to_all.178 = bf16[128,8,512]{2,0,1:T(8,128)(2,1)} all-to-all(bf16[128,8,512]{2,0,1:T(8,128)(2,1)} %bitcast.239), channel_id=1, replica_groups=mesh['rep'=16,'shard'=8] {'shard'}, dimensions={1} | all-to-all | bytes 2097152 | tf_op jit(solution)/shard_map/all_to_all | solution.py:232
  885.5 183.6 %all-gather.15.cloned.1.call-done = bf16[1024,9216]{1,0:T(8,128)(2,1)} async-done(((bf16[128,9216]{1,0:T(8,128)(2,1)}), bf16[1024,9216]{1,0:T(8,128)(2,1)}) %all-gather.15.cloned.1.call-update) | async-done | bytes 18874384 | tf_op jit(solution)/shard_map/all_gather | solution.py:15
  1071.8 203.1 %all-gather.17.cloned.1.call-done = bf16[1024,9216]{1,0:T(8,128)(2,1)} async-done(((bf16[128,9216]{1,0:T(8,128)(2,1)}), bf16[1024,9216]{1,0:T(8,128)(2,1)}) %all-gather.17.cloned.1.call-update) | async-done | bytes 18874384 | tf_op jit(solution)/shard_map/all_gather | solution.py:15
  1355.2 28.3 %all-reduce = (bf16[1,128,2]{1,2,0:T(2,128)(2,1)S(1)}, bf16[1,128,2]{1,2,0:T(2,128)(2,1)S(1)}, bf16[1,128,6]{1,2,0:T(8,128)(2,1)S(1)}, bf16[1,128,6]{1,2,0:T(8,1...) all-reduce(bf16[1,128,2]{1,2,0:T(2,128)(2,1)S(1)} %slice_bitcast_fu, ...), channel_id=1, replica_groups=mesh['rep'=16,'shard'=8] {'rep'}, use_global_device_ids=true, to_apply=%region_49.50 | all-reduce | flops 3072 | bytes 12288 | tf_op jit(solution)/shard_map/psum | solution.py:250
  1385.2 52.9 %all-reduce.4.cloned.1.call-done = (bf16[1,128,3072]{2,1,0:T(8,128)(2,1)}, bf16[1,128,3072]{2,1,0:T(8,128)(2,1)}, bf16[1,128,1024]{2,1,0:T(8,128)(2,1)}, bf16[1,...) async-done(((bf16[1,128,3072]{2,1,0:T(8,128)(2,1)}, ...) | async-done | bytes 6291472 | tf_op jit(solution)/shard_map/psum | solution.py:246
  (376 shorter events, 242.1 us)
Async XLA Ops:
  7.2 296.5 %all-gather.11.cloned.1.call-start = ((), (), s32[]{:S(2)}) async-start(), calls=%async_computation.14 | async-start | bytes 18874368 | tf_op jit(solution)/shard_map/all_gather | solution.py:15
  11.8 478.2 %all-gather.13.cloned.1.call-start = ((), (), s32[]{:S(2)}) async-start(), calls=%async_computation.15 | async-start | bytes 18874368 | tf_op jit(solution)/shard_map/all_gather | solution.py:15
  13.3 585.8 %all-gather.19.cloned.1.call-start = ((), (), s32[]{:S(2)}) async-start(), calls=%async_computation.18 | async-start | bytes 9437184 | tf_op jit(solution)/shard_map/all_gather | solution.py:221
  21.2 204.9 %copy-start.79 = (bf16[2,128,2]{1,2,0:T(2,128)(2,1)S(1)}, bf16[2,128,2]{1,2,0:T(2,128)(2,1)}, u32[]{:S(2)}) copy-start(bf16[2,128,2]{1,2,0:T(2,128)(2,1)} %param.17) | copy-start | bytes 3076
  21.2 298.4 %all-to-all-start = ((bf16[8,512,1024]{2,1,0:T(8,128)(2,1)}), bf16[8,512,1024]{2,1,0:T(8,128)(2,1)}, u32[]{:S(2)}, u32[]{:S(2)}) async-start(bf16[8,512,1024]{2,1,0:T(8,128)(2,1)} %stack.156), calls=%async_computation | async-start | bytes 16777216 | tf_op jit(solution)/shard_map/all_to_all | solution.py:206
  28.3 257.7 %copy-start.74 = (s32[128]{0:T(128)S(1)}, s32[128]{0:T(128)}, u32[]{:S(2)}) copy-start(s32[128]{0:T(128)} %param.11) | copy-start | bytes 1540
  28.4 257.9 %copy-start.23 = (f32[128,1024]{1,0:T(8,128)S(1)}, f32[128,1024]{1,0:T(8,128)}, u32[]{:S(2)}) copy-start(f32[128,1024]{1,0:T(8,128)} %param.12) | copy-start | bytes 1572868
  28.4 679.8 %all-gather.21.cloned.1.call-start = ((), (), s32[]{:S(2)}) async-start(), calls=%async_computation.19 | async-start | bytes 9437184 | tf_op jit(solution)/shard_map/all_gather | solution.py:221
  28.9 1040.1 %all-gather.15.cloned.1.call-start = ((), (), s32[]{:S(2)}) async-start(), calls=%async_computation.16 | async-start | bytes 21233664 | tf_op jit(solution)/shard_map/all_gather | solution.py:15
  742.5 532.4 %all-gather.17.cloned.1.call-start = ((), (), s32[]{:S(2)}) async-start(), calls=%async_computation.17 | async-start | bytes 21233664 | tf_op jit(solution)/shard_map/all_gather | solution.py:15
  746.8 11.9 all-to-all-start.6
  758.7 13.5 all-to-all-start.7
  772.2 14.5 all-to-all-start.4
  786.8 14.2 all-to-all-start.5
  801.0 12.9 all-to-all-start.2
  813.9 13.9 all-to-all-start.3
  827.8 28.6 %all-to-all-start.8 = ((bf16[128,8,512]{2,0,1:T(8,128)(2,1)}), bf16[128,8,512]{2,0,1:T(8,128)(2,1)}, u32[]{:S(2)}, u32[]{:S(2)}) async-start(bf16[128,8,512]{2,0,1:T(8,128)(2,1)} %bitcast.238), calls=%async_computation.8 | async-start | bytes 2097152 | tf_op jit(solution)/shard_map/all_to_all | solution.py:232
  880.3 426.2 %all-to-all-start.1 = ((bf16[8,512,1024]{2,1,0:T(8,128)(2,1)}), bf16[8,512,1024]{2,1,0:T(8,128)(2,1)}, u32[]{:S(2)}, u32[]{:S(2)}) async-start(bf16[8,512,1024]{2,1,0:T(8,128)(2,1)} %stack.157), calls=%async_computation.1 | async-start | bytes 16777216 | tf_op jit(solution)/shard_map/all_to_all | solution.py:206
  885.2 389.7 %copy-start.35 = (bf16[128,8,128]{2,0,1:T(8,128)(2,1)S(1)}, bf16[128,8,128]{2,0,1:T(8,128)(2,1)}, u32[]{:S(2)}) copy-start(bf16[128,8,128]{2,0,1:T(8,128)(2,1)} %copy-done.34) | copy-start | bytes 786436
  885.2 552.9 %all-reduce.4.cloned.1.call-start = ((), (), s32[]{:S(2)}) async-start(), calls=%async_computation.20 | async-start | bytes 12582912 | tf_op jit(solution)/shard_map/psum | solution.py:246
  1306.4 12.0 all-to-all-start.12
  1318.4 14.8 %all-to-all-start.13 = ((bf16[8,2,256]{2,1,0:T(2,128)(2,1)}), bf16[8,2,256]{2,1,0:T(2,128)(2,1)S(1)}, u32[]{:S(2)}, u32[]{:S(2)}) async-start(bf16[8,2,256]{2,1,0:T(2,128)(2,1)} %reshape.410), calls=%async_computation.13 | async-start | bytes 16384 | tf_op jit(solution)/shard_map/all_to_all | solution.py:30
  1333.2 11.0 all-to-all-start.10
  1344.1 11.0 all-to-all-start.11
  (77 other events, 1526.8 us)
Sparse Core Ops, SparseCore 0:
  11.9 291.7 all-gather.10
  306.0 183.8 all-gather.12
  492.3 106.7 all-gather.18
  601.3 106.7 all-gather.20
  742.6 326.3 all-gather.14
  1071.8 203.0 all-gather.16
  1302.5 135.5 all-reduce.3
